TPU v7x, 32 devices: a whole 2x2x4 slice. The times are simulated.
32 devices in a mesh: req: 8 (over z, y), tp: 4 (over x, core).
Axes of the slice: x: 2, y: 2, z: 4, core: 2. Of those that a mesh axis runs over, the one named last changes fastest.
Arguments:
- tokens: bfloat16 [4096, 2048], P('req')
- token_request_number: int32 [8, 512], P('req'), may hold values from 0 to 7, never falling along the last dimension, each value on 1 to 256 neighbouring positions
- request_adapter_position: int32 [8, 8], P('req'), may hold values from 0 to 15
- adapters_in_use: int32 [16], replicated, may hold values from 0 to 15, as said below
- adapter_storage_slot: int32 [16], replicated, may hold values from 0 to 15, each once
- input_norm_gain: bfloat16 [2048], replicated, may hold values from 0.5 to 1.5
- query_weight: bfloat16 [2048, 2048], P('req', 'tp')
- key_weight: bfloat16 [2048, 2048], P('req', 'tp')
- value_weight: bfloat16 [2048, 2048], P('req', 'tp'), may hold values from -0.125 to 0.125
- output_weight: bfloat16 [2048, 2048], P('tp', 'req'), may hold values from -0.125 to 0.125
- adapter_down_weight: bfloat16 [16, 2, 16, 2048], P('req'), may hold values from -0.125 to 0.125
- adapter_up_weight: bfloat16 [16, 2, 16, 2048], P('req', None, None, 'tp'), may hold values from -0.75 to 0.75
Outputs:
- layer_out: bfloat16 [4096, 2048], P('req', 'tp')
Inputs may be any that keep to these rules, and one draw needn't show every extreme that they name: `adapters_in_use`: 16 different adapter numbers; 0 and 15 are always among them. `token_request_number`: the 512 tokens of each index of req form exactly 8 requests in order, each of 1 to 256 tokens, and one of exactly 256.
All inputs are finite; a program needn't handle non-finite values.
Results may differ from a plain program's by a relative error of at most 0.01.
Values may be sent and summed in bfloat16 or wider, within the bound.
A program may use at most 64 MiB of HBM per device.

v0:
```python
import jax
import jax.numpy as jnp
from jax import lax
from jax.sharding import PartitionSpec as P

HEAD_WIDTH = 64
norm_eps = 1e-05
rope_base = 130000.0
adapter_scale = 2.0


def fetch_adapters(down_part, up_part, active_slots, request_adapters, req_total):
    slot_total = down_part.shape[0]
    stored = jnp.concatenate([down_part, up_part], axis=1)
    split = down_part.shape[1]
    if slot_total * req_total <= 2 * active_slots.shape[0]:
        fetched = lax.all_gather(stored, "req", axis=0, tiled=True)
        places = active_slots[request_adapters]
    else:
        own = active_slots // slot_total == lax.axis_index("req")
        rows = jnp.where(
            own[:, None],
            jnp.take(stored, active_slots % slot_total, axis=0),
            jnp.zeros((), stored.dtype),
        )
        fetched = lax.psum(rows, "req")
        places = request_adapters
    return (fetched[:, :split], fetched[:, split:], places)


def positions_of(segment):
    ordinal = jnp.arange(segment.shape[0], dtype=jnp.int32)
    starts = jnp.concatenate([jnp.ones((1,), jnp.bool_), segment[1:] != segment[:-1]])
    segment_start = lax.cummax(jnp.where(starts, ordinal, jnp.zeros_like(ordinal)), axis=0)
    return ordinal - segment_start


def apply_rotation(values, token_positions):
    half_dim = HEAD_WIDTH // 2
    frequency = rope_base ** (-(jnp.arange(half_dim, dtype=jnp.float32) * 2.0 / HEAD_WIDTH))
    angles = token_positions.astype(jnp.float32)[:, None] * frequency[None, :]
    cosine = jnp.cos(angles)[:, None, :]
    sine_part = jnp.sin(angles)[:, None, :]
    first_half = values[..., :half_dim]
    second_half = values[..., half_dim:]
    return jnp.concatenate(
        [
            first_half * cosine - second_half * sine_part,
            second_half * cosine + first_half * sine_part,
        ],
        axis=-1,
    )


def attend(query_per_head, key_heads, value_per_head, segment):
    scores = (
        jnp.einsum("qhd,khd->hqk", query_per_head, key_heads, preferred_element_type=jnp.float32)
        * 0.125
    )
    ordinal = jnp.arange(segment.shape[0], dtype=jnp.int32)
    allowed = (segment[:, None] == segment[None, :]) & (ordinal[None, :] <= ordinal[:, None])
    scores = jnp.where(allowed[None], scores, jnp.float32(-1e30))
    row_peak = jnp.max(scores, axis=-1, keepdims=True)
    exponent = jnp.where(allowed[None], jnp.exp(scores - row_peak), jnp.float32(0.0))
    weights = (exponent / jnp.sum(exponent, axis=-1, keepdims=True)).astype(jnp.bfloat16)
    return jnp.einsum(
        "hqk,khd->qhd", weights, value_per_head, preferred_element_type=jnp.float32
    ).astype(jnp.bfloat16)


def local(
    tokens,
    token_request_number,
    request_adapter_position,
    adapters_in_use,
    adapter_storage_slot,
    input_norm_gain,
    query_weight,
    key_weight,
    value_weight,
    output_weight,
    adapter_down_weight,
    adapter_up_weight,
):
    row_total, model_width = tokens.shape
    local_width = query_weight.shape[1]
    reduced_rows = adapter_down_weight.shape[2]
    active_count = adapters_in_use.shape[0]
    slot_total = adapter_down_weight.shape[0]
    segment = token_request_number[0]
    request_adapters = request_adapter_position[0]
    tp_total = lax.axis_size("tp")
    req_total = lax.axis_size("req")
    part_rows = reduced_rows // tp_total
    down_part = lax.dynamic_slice_in_dim(
        adapter_down_weight, lax.axis_index("tp") * part_rows, part_rows, 2
    ).reshape(slot_total, 2 * part_rows * model_width)
    up_part = adapter_up_weight.reshape(slot_total, 2 * reduced_rows * local_width)
    down_all, up_all, request_places = fetch_adapters(
        down_part,
        up_part,
        jnp.take(adapter_storage_slot, adapters_in_use, axis=0),
        request_adapters,
        req_total,
    )
    place_total = down_all.shape[0]
    floats = tokens.astype(jnp.float32)
    normed = (
        floats
        * lax.rsqrt(jnp.mean(floats * floats, axis=-1, keepdims=True) + norm_eps)
        * input_norm_gain.astype(jnp.float32)
    ).astype(jnp.bfloat16)
    query_plain = jnp.dot(
        normed,
        lax.all_gather(query_weight, "req", axis=0, tiled=True),
        preferred_element_type=jnp.float32,
    )
    key_base = jnp.dot(
        normed,
        lax.all_gather(key_weight, "req", axis=0, tiled=True),
        preferred_element_type=jnp.float32,
    )
    value_plain = jnp.dot(
        normed,
        lax.all_gather(value_weight, "req", axis=0, tiled=True),
        preferred_element_type=jnp.float32,
    )
    request_total = request_adapters.shape[0]
    member = segment[:, None] == jnp.arange(request_total, dtype=jnp.int32)[None, :]
    token_place = jnp.sum(
        jnp.where(member, request_places[None, :], jnp.zeros_like(request_places)[None, :]), axis=1
    )
    share = 2 * part_rows
    shrunk_all = lax.dot_general(
        normed,
        down_all.reshape(place_total * share, model_width),
        (((1,), (1,)), ((), ())),
        preferred_element_type=jnp.float32,
    ).astype(jnp.bfloat16)
    column = jnp.arange(place_total * share, dtype=jnp.int32)
    kept = jnp.where(
        token_place[:, None] == (column // share)[None, :], shrunk_all, jnp.zeros((), jnp.bfloat16)
    )
    fold = (column % share)[:, None] == jnp.arange(share, dtype=jnp.int32)[None, :]
    shrunk_part = jnp.dot(
        kept, fold.astype(jnp.bfloat16), preferred_element_type=jnp.float32
    ).astype(jnp.bfloat16)
    shrunk = lax.all_gather(shrunk_part, "tp", axis=1, tiled=True)
    source = jnp.arange(tp_total * share, dtype=jnp.int32)
    source_kind = source % share // part_rows
    source_rank = source // share * part_rows + source % part_rows
    target = jnp.arange(place_total * reduced_rows, dtype=jnp.int32)
    mine = token_place[:, None] == (target // reduced_rows)[None, :]
    up_all = up_all.reshape(place_total, 2, reduced_rows, local_width)

    def change_of(kind):
        spread_map = (source_kind == kind)[:, None] & (
            source_rank[:, None] == (target % reduced_rows)[None, :]
        )
        spread = jnp.dot(
            shrunk, spread_map.astype(jnp.bfloat16), preferred_element_type=jnp.float32
        ).astype(jnp.bfloat16)
        spread = jnp.where(mine, spread, jnp.zeros((), jnp.bfloat16))
        return jnp.dot(
            spread,
            up_all[:, kind].reshape(place_total * reduced_rows, local_width),
            preferred_element_type=jnp.float32,
        )

    query_change = change_of(0)
    value_change = change_of(1)
    head_total = local_width // HEAD_WIDTH
    token_positions = positions_of(segment)
    query_per_head = apply_rotation(
        (query_plain + adapter_scale * query_change).reshape(row_total, head_total, HEAD_WIDTH),
        token_positions,
    ).astype(jnp.bfloat16)
    key_heads = apply_rotation(
        key_base.reshape(row_total, head_total, HEAD_WIDTH), token_positions
    ).astype(jnp.bfloat16)
    value_per_head = (
        (value_plain + adapter_scale * value_change)
        .astype(jnp.bfloat16)
        .reshape(row_total, head_total, HEAD_WIDTH)
    )
    attended = attend(query_per_head, key_heads, value_per_head, segment).reshape(
        row_total, local_width
    )
    partial_out = jnp.dot(
        attended,
        lax.all_gather(output_weight, "req", axis=1, tiled=True),
        preferred_element_type=jnp.float32,
    )
    summed = lax.psum_scatter(
        partial_out.astype(jnp.bfloat16), "tp", scatter_dimension=1, tiled=True
    ).astype(jnp.float32)
    share_width = summed.shape[1]
    residual_part = lax.dynamic_slice_in_dim(
        tokens, lax.axis_index("tp") * share_width, share_width, 1
    )
    return (summed + residual_part.astype(jnp.float32)).astype(jnp.bfloat16)


def solution(mesh):
    in_specs = (
        P("req", None),
        P("req", None),
        P("req", None),
        P(),
        P(),
        P(),
        P("req", "tp"),
        P("req", "tp"),
        P("req", "tp"),
        P("tp", "req"),
        P("req", None, None, None),
        P("req", None, None, "tp"),
    )
    out_specs = P("req", "tp")
    return jax.shard_map(local, mesh=mesh, in_specs=in_specs, out_specs=out_specs, check_vma=False)
```

profile of v0, /device:TPU:0, one launch (start us, length us, event | category | flops | bytes accessed | tf_op | source)
XLA Modules:
  0.0 296.7 jit_solution(14154784594400048160)
XLA Ops:
  6.5 0.0 copy-start
  6.5 0.0 copy-start.6
  6.5 0.0 copy-start.1
  6.5 0.0 all-gather.15.cloned.1.call-start
  6.6 1.0 copy.18
  7.6 0.0 copy-done
  7.7 0.1 reshape.292
  7.7 0.8 maximum_bitcast_fusion
  8.5 0.0 all-gather.15.cloned.1.call-update
  8.5 0.0 all-gather.7.cloned.1.call-start
  8.6 0.7 all-gather.7.cloned.1.call-update
  9.3 0.0 all-gather.9.cloned.1.call-start
  9.3 0.7 all-gather.9.cloned.1.call-update
  10.0 0.0 all-gather.11.cloned.1.call-start
  10.1 0.5 all-gather.11.cloned.1.call-update
  10.6 0.0 all-gather.13.cloned.1.call-start
  10.6 0.5 all-gather.13.cloned.1.call-update
  11.2 0.0 reduce-scatter.2.cloned.1.call-start
  11.3 0.7 convert_element_type.59
  12.0 2.1 fusion.2
  14.1 0.7 compare_select_fusion.1
  14.8 0.0 copy-done.1
  14.8 0.7 gather_fusion
  15.4 0.0 copy-done.6
  15.4 0.0 copy-start.2
  15.5 0.0 copy-done.7
  15.5 0.0 copy-done.5
  15.5 0.1 compare_reduce_fusion
  15.6 0.9 fusion.18
  16.5 0.6 gather_fusion.1
  17.1 0.1 select_reduce_fusion
  17.2 0.1 add_select_fusion
  17.3 0.3 reduce-window.9
  17.6 0.1 slice.46
  17.7 0.1 slice_reduce_fusion
  17.8 0.1 fusion.47
  17.9 0.9 multiply_cosine_fusion
  18.9 33.5 %all-gather.15.cloned.1.call-done = bf16[8,2,32768]{2,1,0:T(2,128)(2,1)} async-done(((bf16[1,2,32768]{2,1,0:T(2,128)(2,1)}), bf16[8,2,32768]{2,1,0:T(2,128)(2,1)}) %all-gather.15.cloned.1.call-update) | async-done | bytes 1048592 | tf_op jit(solution)/shard_map/all_gather | solution.py:17
  52.4 1.5 reshape.319
  53.9 0.9 fusion.70
  54.7 0.2 copy.19
  54.9 0.9 fusion.71
  55.8 1.3 reshape.294
  57.0 0.0 copy-done.2
  57.0 0.9 fusion.17
  58.0 5.4 %all_gather.20 = bf16[512,32]{0,1:T(8,128)(2,1)S(1)} all-gather(bf16[512,8]{0,1:T(8,128)(2,1)S(1)} %fusion.17), channel_id=1, replica_groups=mesh['req'=8,'tp'=4] {'tp'}, dimensions={1}, use_global_device_ids=true | all-gather | bytes 40960 | tf_op jit(solution)/shard_map/all_gather | solution.py:148
  63.4 39.2 %all-gather.7.cloned.1.call-done = bf16[2048,512]{1,0:T(8,128)(2,1)} async-done(((bf16[256,512]{1,0:T(8,128)(2,1)}), bf16[2048,512]{1,0:T(8,128)(2,1)}) %all-gather.7.cloned.1.call-update) | async-done | bytes 2097168 | tf_op jit(solution)/shard_map/all_gather | solution.py:125
  102.6 3.0 %fusion.68 = f32[512,512]{0,1:T(8,128)S(1)} fusion(bf16[2048,512]{1,0:T(8,128)(2,1)} %all-gather.7.cloned.1.call-done, bf16[512,2048]{1,0:T(8,128)(2,1)S(1)} %copy-done.2, f32[2048]{0:T(1024)S(1)} %convert_element_type.59, f32[512]{0:T(512)S(1)} %add_rsqrt_fusion), kind=kOutput, calls=%fused_computation.120 | convolution fusion | flops 1077936128 | bytes 5253120 | tf_op jit(solution)/shard_map/dot_general | solution.py:123
  105.6 2.3 fusion.12
  107.9 44.7 %all-gather.9.cloned.1.call-done = bf16[2048,512]{1,0:T(8,128)(2,1)} async-done(((bf16[256,512]{1,0:T(8,128)(2,1)}), bf16[2048,512]{1,0:T(8,128)(2,1)}) %all-gather.9.cloned.1.call-update) | async-done | bytes 2097168 | tf_op jit(solution)/shard_map/all_gather | solution.py:115
  152.5 3.9 %fusion.64 = f32[512,512]{0,1:T(8,128)} fusion(bf16[2048,512]{1,0:T(8,128)(2,1)} %all-gather.9.cloned.1.call-done, bf16[512,2048]{1,0:T(8,128)(2,1)S(1)} %copy-done.2, f32[2048]{0:T(1024)S(1)} %convert_element_type.59, f32[512]{0:T(512)S(1)} %add_rsqrt_fusion), kind=kOutput, calls=%fused_computation.119 | convolution fusion | flops 1077936128 | bytes 5253120 | tf_op jit(solution)/shard_map/dot_general | solution.py:113
  156.5 1.9 fusion.9
  158.4 44.0 %all-gather.11.cloned.1.call-done = bf16[2048,512]{1,0:T(8,128)(2,1)} async-done(((bf16[256,512]{1,0:T(8,128)(2,1)}), bf16[2048,512]{1,0:T(8,128)(2,1)}) %all-gather.11.cloned.1.call-update) | async-done | bytes 2097168 | tf_op jit(solution)/shard_map/all_gather | solution.py:120
  202.3 3.0 %fusion.62 = f32[512,512]{0,1:T(8,128)S(1)} fusion(bf16[2048,512]{1,0:T(8,128)(2,1)} %all-gather.11.cloned.1.call-done, bf16[512,2048]{1,0:T(8,128)(2,1)S(1)} %copy-done.2, f32[2048]{0:T(1024)S(1)} %convert_element_type.59, f32[512]{0:T(512)S(1)} %add_rsqrt_fusion), kind=kOutput, calls=%fused_computation.118 | convolution fusion | flops 1077936128 | bytes 5253120 | tf_op jit(solution)/shard_map/dot_general | solution.py:118
  205.3 0.0 copy-done.4
  205.4 1.3 subtract_convert_fusion.1
  206.7 8.2 %fusion.72 = (f32[8,512]{1,0:T(8,128)S(1)}, f32[8,512,512]{1,2,0:T(8,128)}) fusion(pred[512,512]{0,1:T(8,128)(4,1)} %fusion.18, bf16[512,8,32]{0,2,1:T(8,128)(2,1)} %get-tuple-element.13, bf16[512,8,32]{0,2,1:T(8,128)(2,1)} %get-tuple-element.14, bf16[512,8,32]{0,2,1:T(8,128)(2,1)} %get-tuple-element.6, bf16[512,8,32]{0,2,1:T(8,128)(2,1)} %get-tuple-element.5), kind=kOutput, calls=%fused_computation.123 | convolution fusion | flops 281018880 | bytes 9715712 | tf_op jit(solution)/shard_map/sub | solution.py:64
  214.9 0.0 copy-done.3
  214.9 4.3 %fusion.11 = bf16[8,64,512]{2,1,0:T(8,128)(2,1)S(1)} fusion(bf16[512,8,64]{0,2,1:T(8,128)(2,1)S(1)} %bitcast.46, f32[8,512,512]{1,2,0:T(8,128)} %get-tuple-element.18, f32[8,512]{1,0:T(8,128)S(1)} %get-tuple-element.17), kind=kOutput, calls=%fused_computation.21 | convolution fusion | flops 272891904 | bytes 9453568 | tf_op jit(solution)/shard_map/hqk,khd->qhd/dot_general | solution.py:66
  219.2 34.7 %all-gather.13.cloned.1.call-done = bf16[512,2048]{1,0:T(8,128)(2,1)} async-done(((bf16[512,256]{1,0:T(8,128)(2,1)}), bf16[512,2048]{1,0:T(8,128)(2,1)}) %all-gather.13.cloned.1.call-update) | async-done | bytes 2097168 | tf_op jit(solution)/shard_map/all_gather | solution.py:191
  253.8 4.2 %convolution_convert_fusion = bf16[512,2048]{1,0:T(8,128)(2,1)} fusion(bf16[512,512]{0,1:T(8,128)(2,1)S(1)} %bitcast.51, bf16[512,2048]{1,0:T(8,128)(2,1)} %all-gather.13.cloned.1.call-done), kind=kOutput, calls=%fused_computation.16 | convolution fusion | flops 1074790400 | bytes 4718592 | tf_op jit(solution)/shard_map/dot_general | solution.py:189
  258.0 0.0 reduce-scatter.2.cloned.1.call-update
  258.1 29.8 %reduce-scatter.2.cloned.1.call-done = bf16[512,512]{1,0:T(8,128)(2,1)} async-done(((bf16[512,2048]{1,0:T(8,128)(2,1)}), bf16[512,512]{1,0:T(8,128)(2,1)}) %reduce-scatter.2.cloned.1.call-update) | async-done | bytes 524304 | tf_op jit(solution)/shard_map/reduce_scatter | solution.py:194
  287.8 2.0 add_convert_fusion
  (17 shorter events, 0.2 us)
Async XLA Ops:
  6.5 1.1 copy-start
  6.5 8.9 %copy-start.6 = (s32[16]{0:T(128)S(1)}, s32[16]{0:T(128)}, u32[]{:S(2)}) copy-start(s32[16]{0:T(128)} %param.15) | copy-start | bytes 196
  6.5 8.2 %copy-start.1 = (s32[16]{0:T(128)S(1)}, s32[16]{0:T(128)}, u32[]{:S(2)}) copy-start(s32[16]{0:T(128)} %param.16) | copy-start | bytes 196
  6.5 8.9 %copy-start.7 = (s32[1,8]{1,0:T(1,128)S(1)}, s32[1,8]{1,0:T(1,128)}, u32[]{:S(2)}) copy-start(s32[1,8]{1,0:T(1,128)} %param.14) | copy-start | bytes 100
  6.5 8.9 %copy-start.5 = (s32[1,512]{1,0:T(1,128)S(1)}, s32[1,512]{1,0:T(1,128)}, u32[]{:S(2)}) copy-start(s32[1,512]{1,0:T(1,128)} %param.13) | copy-start | bytes 6148
  6.5 45.8 %all-gather.15.cloned.1.call-start = ((), (), s32[]{:S(2)}) async-start(), calls=%async_computation.6 | async-start | bytes 1179648 | tf_op jit(solution)/shard_map/all_gather | solution.py:17
  8.5 94.1 %all-gather.7.cloned.1.call-start = ((), (), s32[]{:S(2)}) async-start(), calls=%async_computation.1 | async-start | bytes 2359296 | tf_op jit(solution)/shard_map/all_gather | solution.py:125
  9.3 143.3 %all-gather.9.cloned.1.call-start = ((), (), s32[]{:S(2)}) async-start(), calls=%async_computation.2 | async-start | bytes 2359296 | tf_op jit(solution)/shard_map/all_gather | solution.py:115
  10.0 192.3 %all-gather.11.cloned.1.call-start = ((), (), s32[]{:S(2)}) async-start(), calls=%async_computation.3 | async-start | bytes 2359296 | tf_op jit(solution)/shard_map/all_gather | solution.py:120
  10.6 243.2 %all-gather.13.cloned.1.call-start = ((), (), s32[]{:S(2)}) async-start(), calls=%async_computation.4 | async-start | bytes 2359296 | tf_op jit(solution)/shard_map/all_gather | solution.py:191
  11.2 276.6 %reduce-scatter.2.cloned.1.call-start = ((), (), s32[]{:S(2)}) async-start(), calls=%async_computation.5 | async-start | bytes 2621440 | tf_op jit(solution)/shard_map/reduce_scatter | solution.py:194
  15.4 41.6 %copy-start.2 = (bf16[512,2048]{1,0:T(8,128)(2,1)S(1)}, bf16[512,2048]{1,0:T(8,128)(2,1)}, u32[]{:S(2)}) copy-start(bf16[512,2048]{1,0:T(8,128)(2,1)} %param.12) | copy-start | bytes 6291460
  202.3 3.0 %copy-start.4 = (f32[512,32]{0,1:T(8,128)S(1)}, f32[512,32]{0,1:T(8,128)}, u32[]{:S(2)}) copy-start(f32[512,32]{0,1:T(8,128)} %get-tuple-element.16) | copy-start | bytes 196612
  206.7 8.2 %copy-start.3 = (bf16[512,512]{0,1:T(8,128)(2,1)S(1)}, bf16[512,512]{0,1:T(8,128)(2,1)}, u32[]{:S(2)}) copy-start(bf16[512,512]{0,1:T(8,128)(2,1)} %fusion.12) | copy-start | bytes 1572868
Sparse Core Ops, SparseCore 0:
  9.5 42.8 all-gather.14
  54.5 48.0 all-gather.6
  104.7 47.7 all-gather.8
  154.5 47.7 all-gather.10
  204.2 49.5 all-gather.12
  258.2 29.5 reduce-scatter.1
where the time goes:
time: 297 us
  waiting for transfers between devices  228 us (77%)
  matrix products  31.7 us (11%)
  between operations  13.7 us (5%)
  other arithmetic  10.1 us (3%)
  local copies, waits for them, and re-layouts  7.27 us (2%)
  blocking collectives  5.39 us (2%)
    all_gather x1, waiting for transfers between devices, local(): lax.all_gather(query_weight, 'req', axis=0, tiled=True)  44.7 us
    all_gather x1, waiting for transfers between devices, local(): lax.all_gather(key_weight, 'req', axis=0, tiled=True)  44 us
    all_gather x1, waiting for transfers between devices, local(): lax.all_gather(value_weight, 'req', axis=0, tiled=True)  39.2 us
    all_gather x1, waiting for transfers between devices, local(): lax.all_gather(output_weight, 'req', axis=1, tiled=True)  34.7 us
    all_gather x1, waiting for transfers between devices, fetch_adapters(): fetched = lax.all_gather(stored, 'req', axis=0, tiled=True)  33.5 us
    reduce_scatter x1, waiting for transfers between devices, local(): lax.psum_scatter(partial_out.astype(jnp.bfloat16), 'tp', scatter_dimensio...  29.8 us
    sub x1, matrix products, attend(): scores - row_peak  8.2 us
  transfers between devices with their start and end apart: 6, of which 6 were waited for; matrix products, arithmetic and copies ran while one was open for 14% of the time, Pallas kernels for 0%

commit v1 on v0

--- a/solution.py
+++ b/solution.py
@@ -7,6 +7,28 @@
 norm_eps = 1e-05
 rope_base = 130000.0
 adapter_scale = 2.0
+
+
+def in_order(pieces, dim):
+    shape = list(pieces.shape[1:])
+    shape[dim] *= pieces.shape[0]
+    return jnp.moveaxis(pieces, 0, dim).reshape(shape)
+
+
+def collected_by_bits(shard, axis):
+    devices = lax.axis_size(axis)
+    tiles = shard[None]
+    for level in range(devices.bit_length() - 1):
+        apart = 1 << level
+        partner_block = lax.ppermute(tiles, axis, [(i, i ^ apart) for i in range(devices)])
+        both = jnp.stack([tiles, partner_block])
+        upper = lax.axis_index(axis) >> level & 1
+        tiles = jnp.where(upper == 0, both, both[::-1]).reshape(-1, *shard.shape)
+    return tiles
+
+
+def doubled_up(x, axis, dim):
+    return in_order(collected_by_bits(x, axis), dim)
 
 
 def fetch_adapters(down_part, up_part, active_slots, request_adapters, req_total):
@@ -111,9 +133,7 @@
         * input_norm_gain.astype(jnp.float32)
     ).astype(jnp.bfloat16)
     query_plain = jnp.dot(
-        normed,
-        lax.all_gather(query_weight, "req", axis=0, tiled=True),
-        preferred_element_type=jnp.float32,
+        normed, doubled_up(query_weight, "req", 0), preferred_element_type=jnp.float32
     )
     key_base = jnp.dot(
         normed,

time: 297 us -> 275 us (0.926)
  waiting for transfers between devices: 228 us -> 193 us
  starting transfers between devices: 0.23 us -> 7.6 us
    all_gather x1 -> x0, waiting for transfers between devices: 44.7 us -> none  [local(): lax.all_gather(query_weight, 'req', axis=0, tiled=True)]
    ppermute x0 -> x3, waiting for transfers between devices: none -> 23.3 us  [collected_by_bits(): lax.ppermute(tiles, axis, [(i, i ^ apart) for i in range(devices)])]
    all_gather x1, waiting for transfers between devices: 39.2 us -> 23.4 us  [local(): lax.all_gather(value_weight, 'req', axis=0, tiled=True)]
    ppermute x0 -> x3, starting transfers between devices: none -> 7.45 us  [collected_by_bits(): lax.ppermute(tiles, axis, [(i, i ^ apart) for i in range(devices)])]
    all_gather x1, waiting for transfers between devices: 33.5 us -> 37.1 us  [fetch_adapters(): fetched = lax.all_gather(stored, 'req', axis=0, tiled=True)]
  transfers between devices with their start and end apart: 6 -> 8, of which waited for: 6 -> 8; matrix products, arithmetic and copies ran while one was open for 14% -> 17% of each run, Pallas kernels for 0% -> 0%
where the time goes in v1:
time: 275 us
  waiting for transfers between devices  193 us (70%)
  matrix products  33 us (12%)
  between operations  13.4 us (5%)
  other arithmetic  12.4 us (5%)
  local copies, waits for them, and re-layouts  9.82 us (4%)
  starting transfers between devices  7.6 us (3%)
  blocking collectives  5.39 us (2%)
    all_gather x1, waiting for transfers between devices, local(): lax.all_gather(key_weight, 'req', axis=0, tiled=True)  43.3 us
    all_gather x1, waiting for transfers between devices, fetch_adapters(): fetched = lax.all_gather(stored, 'req', axis=0, tiled=True)  37.1 us
    all_gather x1, waiting for transfers between devices, local(): lax.all_gather(output_weight, 'req', axis=1, tiled=True)  34.7 us
    reduce_scatter x1, waiting for transfers between devices, local(): lax.psum_scatter(partial_out.astype(jnp.bfloat16), 'tp', scatter_dimensio...  29.8 us
    all_gather x1, waiting for transfers between devices, local(): lax.all_gather(value_weight, 'req', axis=0, tiled=True)  23.4 us
    ppermute x3, waiting for transfers between devices, collected_by_bits(): lax.ppermute(tiles, axis, [(i, i ^ apart) for i in range(devices)])  23.3 us
    sub x1, matrix products, attend(): scores - row_peak  8.19 us
    ppermute x3, starting transfers between devices, collected_by_bits(): lax.ppermute(tiles, axis, [(i, i ^ apart) for i in range(devices)])  7.45 us
  transfers between devices with their start and end apart: 8, of which 8 were waited for; matrix products, arithmetic and copies ran while one was open for 17% of the time, Pallas kernels for 0%

profile of v1, /device:TPU:0, one launch (start us, length us, event | category | flops | bytes accessed | tf_op | source)
XLA Modules:
  0.0 274.7 jit_solution(8003591898480120133)
XLA Ops:
  6.6 0.0 copy-start.10
  6.6 0.0 copy-start.7
  6.6 0.9 copy.18
  7.6 0.1 reshape.298
  7.7 0.8 maximum_bitcast_fusion
  8.4 0.0 all-gather.12.cloned.1.call-update
  8.5 0.0 all-gather.6.cloned.1.call-start
  8.5 0.7 all-gather.6.cloned.1.call-update
  9.2 0.0 all-gather.8.cloned.1.call-start
  9.3 0.7 all-gather.8.cloned.1.call-update
  10.0 0.0 all-gather.10.cloned.1.call-start
  10.0 3.0 %collective-permute-start = (bf16[1,256,512]{2,1,0:T(8,128)(2,1)}, bf16[1,256,512]{2,1,0:T(8,128)(2,1)S(1)}, u32[]{:S(2)}, u32[]{:S(2)}) collective-permute-start(bf16[1,256,512]{2,1,0:T(8,128)(2,1)} %bitcast.64), channel_id=1, source_target_pairs={{0,4},{4,0},{8,12},{12,8},{16,20},{20,16},{24,28},{28,24},{1,5},{5... | collective-permute-start | bytes 786440 | tf_op jit(solution)/shard_map/ppermute | solution.py:23
  13.0 0.0 all-gather.10.cloned.1.call-update
  13.1 0.0 reduce-scatter.2.cloned.1.call-start
  13.2 2.1 fusion.2
  15.3 0.7 gather_fusion
  16.0 0.1 compare_reduce_fusion
  16.1 0.1 add_select_fusion
  16.2 0.3 reduce-window.9
  16.5 0.1 slice.46
  16.6 0.1 slice_reduce_fusion
  16.7 0.6 gather_fusion.1
  17.4 0.1 select_reduce_fusion
  17.5 0.1 fusion.48
  17.6 2.0 collective-permute-done
  19.6 0.1 pad_maximum_fusion.2
  19.6 0.1 fusion.23
  19.7 1.9 collective-permute-start.1
  21.6 0.9 multiply_cosine_fusion
  22.6 0.9 fusion.17
  23.5 13.7 %collective-permute-done.1 = bf16[2,256,512]{2,1,0:T(8,128)(2,1)S(1)} collective-permute-done((bf16[2,256,512]{2,1,0:T(8,128)(2,1)S(1)}, bf16[2,256,512]{2,1,0:T(8,128)(2,1)S(1)}, u32[]{:S(2)}, u32[]{:S(2)}) %collective-permute-start.1) | collective-permute-done | bytes 524320 | tf_op jit(solution)/shard_map/ppermute | solution.py:23
  37.1 0.1 pad_maximum_fusion.1
  37.2 0.2 reverse_select_fusion.1
  37.4 2.6 collective-permute-start.2
  40.0 37.1 %all-gather.12.cloned.1.call-done = bf16[8,2,32768]{2,1,0:T(2,128)(2,1)} async-done(((bf16[1,2,32768]{2,1,0:T(2,128)(2,1)}), bf16[8,2,32768]{2,1,0:T(2,128)(2,1)}) %all-gather.12.cloned.1.call-update) | async-done | bytes 1048592 | tf_op jit(solution)/shard_map/all_gather | solution.py:39
  77.1 1.5 reshape.327
  78.5 0.9 fusion.70
  79.4 1.0 copy.19
  80.4 2.1 reshape.300
  82.5 0.0 copy-done.2
  82.5 2.0 fusion.16
  84.4 5.4 %all_gather.17 = bf16[512,32]{0,1:T(8,128)(2,1)S(1)} all-gather(bf16[512,8]{0,1:T(8,128)(2,1)S(1)} %fusion.16), channel_id=1, replica_groups=mesh['req'=8,'tp'=4] {'tp'}, dimensions={1}, use_global_device_ids=true | all-gather | bytes 40960 | tf_op jit(solution)/shard_map/all_gather | solution.py:168
  89.8 1.8 fusion.71
  91.7 7.6 %collective-permute-done.2 = bf16[4,256,512]{2,1,0:T(8,128)(2,1)} collective-permute-done((bf16[4,256,512]{2,1,0:T(8,128)(2,1)S(1)}, bf16[4,256,512]{2,1,0:T(8,128)(2,1)}, u32[]{:S(2)}, u32[]{:S(2)}) %collective-permute-start.2) | collective-permute-done | bytes 1048608 | tf_op jit(solution)/shard_map/ppermute | solution.py:23
  99.3 1.4 pad_maximum_fusion
  100.7 0.0 copy-start.3
  100.7 1.8 reverse_select_fusion
  102.5 1.6 convolution_multiply_fusion
  104.0 3.2 %convolution_add_fusion = f32[512,512]{0,1:T(8,128)S(1)} fusion(f32[512,512]{0,1:T(8,128)} %convolution_multiply_fusion, bf16[2048,512]{1,0:T(8,128)(2,1)} %bitcast.54, bf16[512,2048]{1,0:T(8,128)(2,1)S(1)} %copy-done.2, f32[2048]{0:T(1024)S(1)} %convert_element_type.59, f32[512]{0:T(512)S(1)} %add_rsqrt_fusion), kind=kOutput, calls=%fused_computation.23 | convolution fusion | flops 1078198272 | bytes 6301696 | tf_op jit(solution)/shard_map/dot_general | solution.py:135
  107.3 23.4 %all-gather.6.cloned.1.call-done = bf16[2048,512]{1,0:T(8,128)(2,1)} async-done(((bf16[256,512]{1,0:T(8,128)(2,1)}), bf16[2048,512]{1,0:T(8,128)(2,1)}) %all-gather.6.cloned.1.call-update) | async-done | bytes 2097168 | tf_op jit(solution)/shard_map/all_gather | solution.py:145
  130.7 3.9 %fusion.68 = f32[512,512]{0,1:T(8,128)} fusion(bf16[2048,512]{1,0:T(8,128)(2,1)} %all-gather.6.cloned.1.call-done, bf16[512,2048]{1,0:T(8,128)(2,1)S(1)} %copy-done.2, f32[2048]{0:T(1024)S(1)} %convert_element_type.59, f32[512]{0:T(512)S(1)} %add_rsqrt_fusion), kind=kOutput, calls=%fused_computation.127 | convolution fusion | flops 1077936128 | bytes 5253120 | tf_op jit(solution)/shard_map/dot_general | solution.py:143
  134.7 2.7 fusion.11
  137.4 43.3 %all-gather.8.cloned.1.call-done = bf16[2048,512]{1,0:T(8,128)(2,1)} async-done(((bf16[256,512]{1,0:T(8,128)(2,1)}), bf16[2048,512]{1,0:T(8,128)(2,1)}) %all-gather.8.cloned.1.call-update) | async-done | bytes 2097168 | tf_op jit(solution)/shard_map/all_gather | solution.py:140
  180.7 3.0 %fusion.63 = f32[512,512]{0,1:T(8,128)S(1)} fusion(bf16[2048,512]{1,0:T(8,128)(2,1)} %all-gather.8.cloned.1.call-done, bf16[512,2048]{1,0:T(8,128)(2,1)S(1)} %copy-done.2, f32[2048]{0:T(1024)S(1)} %convert_element_type.59, f32[512]{0:T(512)S(1)} %add_rsqrt_fusion), kind=kOutput, calls=%fused_computation.126 | convolution fusion | flops 1077936128 | bytes 5253120 | tf_op jit(solution)/shard_map/dot_general | solution.py:138
  183.7 0.0 copy-done.5
  183.7 1.3 subtract_convert_fusion.1
  185.0 8.2 %fusion.72 = (f32[8,512]{1,0:T(8,128)S(1)}, f32[8,512,512]{1,2,0:T(8,128)}) fusion(pred[512,512]{0,1:T(8,128)(4,1)} %fusion.17, bf16[512,8,32]{0,2,1:T(8,128)(2,1)} %get-tuple-element.15, bf16[512,8,32]{0,2,1:T(8,128)(2,1)} %get-tuple-element.16, bf16[512,8,32]{0,2,1:T(8,128)(2,1)} %get-tuple-element.6, bf16[512,8,32]{0,2,1:T(8,128)(2,1)} %get-tuple-element.5), kind=kOutput, calls=%fused_computation.130 | convolution fusion | flops 281018880 | bytes 9715712 | tf_op jit(solution)/shard_map/sub | solution.py:86
  193.2 0.0 copy-done.4
  193.2 4.2 %fusion.10 = bf16[8,64,512]{2,1,0:T(8,128)(2,1)S(1)} fusion(bf16[512,8,64]{0,2,1:T(8,128)(2,1)S(1)} %bitcast.61, f32[8,512,512]{1,2,0:T(8,128)} %get-tuple-element.20, f32[8,512]{1,0:T(8,128)S(1)} %get-tuple-element.19), kind=kOutput, calls=%fused_computation.24 | convolution fusion | flops 272891904 | bytes 9453568 | tf_op jit(solution)/shard_map/hqk,khd->qhd/dot_general | solution.py:88
  197.5 34.7 %all-gather.10.cloned.1.call-done = bf16[512,2048]{1,0:T(8,128)(2,1)} async-done(((bf16[512,256]{1,0:T(8,128)(2,1)}), bf16[512,2048]{1,0:T(8,128)(2,1)}) %all-gather.10.cloned.1.call-update) | async-done | bytes 2097168 | tf_op jit(solution)/shard_map/all_gather | solution.py:211
  232.2 4.2 %convolution_convert_fusion = bf16[512,2048]{1,0:T(8,128)(2,1)} fusion(bf16[512,512]{0,1:T(8,128)(2,1)S(1)} %bitcast.70, bf16[512,2048]{1,0:T(8,128)(2,1)} %all-gather.10.cloned.1.call-done), kind=kOutput, calls=%fused_computation.17 | convolution fusion | flops 1074790400 | bytes 4718592 | tf_op jit(solution)/shard_map/dot_general | solution.py:209
  236.4 0.0 reduce-scatter.2.cloned.1.call-update
  236.4 29.8 %reduce-scatter.2.cloned.1.call-done = bf16[512,512]{1,0:T(8,128)(2,1)} async-done(((bf16[512,2048]{1,0:T(8,128)(2,1)}), bf16[512,512]{1,0:T(8,128)(2,1)}) %reduce-scatter.2.cloned.1.call-update) | async-done | bytes 524304 | tf_op jit(solution)/shard_map/reduce_scatter | solution.py:214
  266.2 2.0 add_convert_fusion
  (32 shorter events, 0.2 us)
Async XLA Ops:
  6.5 1.0 copy-start
  6.5 8.7 %copy-start.9 = (s32[16]{0:T(128)S(1)}, s32[16]{0:T(128)}, u32[]{:S(2)}) copy-start(s32[16]{0:T(128)} %param.15) | copy-start | bytes 196
  6.5 8.7 %copy-start.1 = (s32[16]{0:T(128)S(1)}, s32[16]{0:T(128)}, u32[]{:S(2)}) copy-start(s32[16]{0:T(128)} %param.16) | copy-start | bytes 196
  6.5 70.5 %all-gather.12.cloned.1.call-start = ((), (), s32[]{:S(2)}) async-start(), calls=%async_computation.5 | async-start | bytes 1179648 | tf_op jit(solution)/shard_map/all_gather | solution.py:39
  6.6 9.4 %copy-start.10 = (s32[1,8]{1,0:T(1,128)S(1)}, s32[1,8]{1,0:T(1,128)}, u32[]{:S(2)}) copy-start(s32[1,8]{1,0:T(1,128)} %param.14) | copy-start | bytes 100
  6.6 9.4 %copy-start.7 = (s32[1,512]{1,0:T(1,128)S(1)}, s32[1,512]{1,0:T(1,128)}, u32[]{:S(2)}) copy-start(s32[1,512]{1,0:T(1,128)} %param.13) | copy-start | bytes 6148
  8.4 9.0 %copy-start.8 = (bf16[2048]{0:T(1024)(128)(2,1)S(1)}, bf16[2048]{0:T(1024)(128)(2,1)}, u32[]{:S(2)}) copy-start(bf16[2048]{0:T(1024)(128)(2,1)} %param.17) | copy-start | bytes 12292
  8.4 11.1 %copy-start.6 = (bf16[256,512]{1,0:T(8,128)(2,1)S(1)}, bf16[256,512]{1,0:T(8,128)(2,1)}, u32[]{:S(2)}) copy-start(bf16[256,512]{1,0:T(8,128)(2,1)} %param.18) | copy-start | bytes 786436
  8.5 122.3 %all-gather.6.cloned.1.call-start = ((), (), s32[]{:S(2)}) async-start(), calls=%async_computation.1 | async-start | bytes 2359296 | tf_op jit(solution)/shard_map/all_gather | solution.py:145
  9.2 171.5 %all-gather.8.cloned.1.call-start = ((), (), s32[]{:S(2)}) async-start(), calls=%async_computation.2 | async-start | bytes 2359296 | tf_op jit(solution)/shard_map/all_gather | solution.py:140
  10.0 222.2 %all-gather.10.cloned.1.call-start = ((), (), s32[]{:S(2)}) async-start(), calls=%async_computation.3 | async-start | bytes 2359296 | tf_op jit(solution)/shard_map/all_gather | solution.py:211
  10.0 9.6 %collective-permute-start = (bf16[1,256,512]{2,1,0:T(8,128)(2,1)}, bf16[1,256,512]{2,1,0:T(8,128)(2,1)S(1)}, u32[]{:S(2)}, u32[]{:S(2)}) collective-permute-start(bf16[1,256,512]{2,1,0:T(8,128)(2,1)} %bitcast.64), channel_id=1, source_target_pairs={{0,4},{4,0},{8,12},{12,8},{16,20},{20,16},{24,28},{28,24},{1,5},{5... | collective-permute-start | bytes 786440 | tf_op jit(solution)/shard_map/ppermute | solution.py:23
  13.1 253.1 %reduce-scatter.2.cloned.1.call-start = ((), (), s32[]{:S(2)}) async-start(), calls=%async_computation.4 | async-start | bytes 2621440 | tf_op jit(solution)/shard_map/reduce_scatter | solution.py:214
  19.7 17.4 %collective-permute-start.1 = (bf16[2,256,512]{2,1,0:T(8,128)(2,1)S(1)}, bf16[2,256,512]{2,1,0:T(8,128)(2,1)S(1)}, u32[]{:S(2)}, u32[]{:S(2)}) collective-permute-start(bf16[2,256,512]{2,1,0:T(8,128)(2,1)S(1)} %get-tuple-element.12), channel_id=1, source_target_pairs={{0,8},{4,12},{8,0},{12,4},{16,24},{20,28},{24,16},{28,20},{1,9},{5... | collective-permute-start | bytes 1572872 | tf_op jit(solution)/shard_map/ppermute | solution.py:23
  37.4 61.8 %collective-permute-start.2 = (bf16[4,256,512]{2,1,0:T(8,128)(2,1)S(1)}, bf16[4,256,512]{2,1,0:T(8,128)(2,1)}, u32[]{:S(2)}, u32[]{:S(2)}) collective-permute-start(bf16[4,256,512]{2,1,0:T(8,128)(2,1)S(1)} %bitcast.52), channel_id=1, source_target_pairs={{0,16},{4,20},{8,24},{12,28},{16,0},{20,4},{24,8},{28,12},{1,17},{... | collective-permute-start | bytes 3145736 | tf_op jit(solution)/shard_map/ppermute | solution.py:23
  79.4 3.0 %copy-start.2 = (bf16[512,2048]{1,0:T(8,128)(2,1)S(1)}, bf16[512,2048]{1,0:T(8,128)(2,1)}, u32[]{:S(2)}) copy-start(bf16[512,2048]{1,0:T(8,128)(2,1)} %param.12) | copy-start | bytes 6291460
  100.7 1.8 copy-start.3
  180.7 3.0 %copy-start.5 = (f32[512,32]{0,1:T(8,128)S(1)}, f32[512,32]{0,1:T(8,128)}, u32[]{:S(2)}) copy-start(f32[512,32]{0,1:T(8,128)} %get-tuple-element.18) | copy-start | bytes 196612
  185.0 8.2 %copy-start.4 = (bf16[512,512]{0,1:T(8,128)(2,1)S(1)}, bf16[512,512]{0,1:T(8,128)(2,1)}, u32[]{:S(2)}) copy-start(bf16[512,512]{0,1:T(8,128)(2,1)} %fusion.11) | copy-start | bytes 1572868
Sparse Core Ops, SparseCore 0:
  9.5 67.5 all-gather.11
  79.2 51.5 all-gather.5
  132.9 47.7 all-gather.7
  182.6 49.5 all-gather.9
  236.5 29.5 reduce-scatter.1
